TPU v7x, 256 devices: a whole 4x4x8 slice. The times are simulated.
256 devices in a mesh: atoms: 4 (over y), frames: 64 (over x, z, core).
Axes of the slice: x: 4, y: 4, z: 8, core: 2. Of those that a mesh axis runs over, the one named last changes fastest.
Arguments:
- frames: float32 [1536, 3, 98304], P('frames', None, 'atoms'), may hold values from -48 to 48
- mean_structure: float32 [3, 98304], P(None, 'atoms'), may hold values from -16 to 16
- atom_weight: float32 [98304], P('atoms'), may hold values from 1 to 32
- subspace: bfloat16 [32, 3, 98304], P(None, None, 'atoms'), may hold values from -6 to 6
Outputs:
- new_mean: float32 [3, 98304], P(None, ('atoms', 'frames'))
- image: float32 [32, 3, 98304], P(None, None, ('atoms', 'frames'))
- basis: float32 [32, 3, 98304], P(None, None, ('atoms', 'frames'))
All inputs are finite; a program needn't handle non-finite values.
Results may differ from a plain program's by a relative error of at most 0.0076.
Values may be sent and summed in bfloat16 or wider, within the bound.
A program may use at most 128 MiB of HBM per device.

v0:
```python
import jax
import jax.numpy as jnp
from jax import lax
from jax.sharding import PartitionSpec as P

A = 98304
NEWTON = 8


def newton_polar(moment):
    norm = jnp.sqrt(jnp.sum(moment * moment, axis=(1, 2)))
    x = moment / norm[:, None, None]
    for step in range(NEWTON):
        x00, x01, x02 = (x[:, 0, 0], x[:, 0, 1], x[:, 0, 2])
        x10, x11, x12 = (x[:, 1, 0], x[:, 1, 1], x[:, 1, 2])
        x20, x21, x22 = (x[:, 2, 0], x[:, 2, 1], x[:, 2, 2])
        c00 = x11 * x22 - x12 * x21
        c01 = x12 * x20 - x10 * x22
        c02 = x10 * x21 - x11 * x20
        c10 = x02 * x21 - x01 * x22
        c11 = x00 * x22 - x02 * x20
        c12 = x01 * x20 - x00 * x21
        c20 = x01 * x12 - x02 * x11
        c21 = x02 * x10 - x00 * x12
        c22 = x00 * x11 - x01 * x10
        determ = x00 * c00 + x01 * c01 + x02 * c02
        cofac = jnp.stack(
            [
                jnp.stack([c00, c01, c02], axis=1),
                jnp.stack([c10, c11, c12], axis=1),
                jnp.stack([c20, c21, c22], axis=1),
            ],
            axis=1,
        )
        x = 0.5 * (x + cofac / determ[:, None, None])
    return x


def per_device(frames, mean_structure, atom_weight, subspace):
    highest = lax.Precision.HIGHEST
    frame_count = frames.shape[0] * lax.axis_size("frames")
    weighted = atom_weight[None, :] * mean_structure
    local_first = jnp.einsum("a,fia->fi", atom_weight, frames, precision=highest)
    total, mean_sum = lax.psum((jnp.sum(atom_weight), jnp.sum(weighted, axis=1)), "atoms")
    mean_center = mean_sum / total
    centered = (mean_structure - mean_center[:, None]) * atom_weight[None, :]
    local_second = jnp.einsum("ia,fja->fij", centered, frames, precision=highest)
    first, second = lax.psum((local_first, local_second), "atoms")
    moment = second / total
    frame_center = first / total
    rotation = newton_polar(moment)
    anchor = mean_center[:, None] - mean_structure
    moved = jnp.einsum("fij,fja->fia", rotation, frames, precision=highest)
    offset = jnp.einsum("fij,fj->fi", rotation, frame_center, precision=highest)
    displaced = (moved - offset[:, :, None] + anchor[None]).astype(jnp.bfloat16)
    frame_rows = displaced.shape[0]
    vectors = subspace.shape[0]
    local_proj = jnp.einsum(
        "fc,kc->fk",
        displaced.reshape(frame_rows, -1),
        subspace.reshape(vectors, -1),
        preferred_element_type=jnp.float32,
    )
    projection = lax.psum(local_proj, "atoms")
    proj_total = lax.psum(jnp.sum(local_proj, axis=0), ("atoms", "frames"))
    centered_projection = (projection - proj_total / frame_count).astype(jnp.bfloat16)
    term = jnp.einsum(
        "fk,fia->kia", centered_projection, displaced, preferred_element_type=jnp.float32
    )
    shift_sum = jnp.sum(displaced, axis=0, dtype=jnp.float32)
    stacked = jnp.concatenate([term, shift_sum[None]], axis=0)
    reduced = lax.psum_scatter(stacked, "frames", scatter_dimension=2, tiled=True)
    image_sum = reduced[:vectors]
    mean_shift = reduced[vectors]
    image = image_sum / frame_count
    width = image.shape[2]
    own_mean = lax.dynamic_slice_in_dim(mean_structure, lax.axis_index("frames") * width, width, 1)
    new_mean = own_mean + mean_shift / frame_count
    flat = image.reshape(vectors, -1)
    gram = lax.psum(jnp.dot(flat, flat.T, precision=highest), ("atoms", "frames")) / (3 * A)
    lower = jnp.linalg.cholesky(gram)
    basis = jax.scipy.linalg.solve_triangular(lower, flat, lower=True)
    return (new_mean, image, basis.reshape(image.shape))


def solution(mesh):
    return jax.shard_map(
        per_device,
        mesh=mesh,
        in_specs=(P("frames", None, "atoms"), P(None, "atoms"), P("atoms"), P(None, None, "atoms")),
        out_specs=(
            P(None, ("atoms", "frames")),
            P(None, None, ("atoms", "frames")),
            P(None, None, ("atoms", "frames")),
        ),
        check_vma=False,
    )
```

profile of v0, /device:TPU:1, one launch (start us, length us, event | category | flops | bytes accessed | tf_op | source)
XLA Modules:
  0.0 459.7 jit_solution(17343104478468763775)
XLA Ops:
  7.2 1.3 multiply_reduce_fusion
  8.6 1.5 reduce_sum.46
  10.1 10.1 %all-reduce.1 = (f32[3]{0:T(128)S(1)}, f32[]{:T(128)}) all-reduce(f32[3]{0:T(128)S(1)} %multiply_reduce_fusion, f32[]{:T(128)} %reduce_sum.46), channel_id=1, replica_groups=mesh['atoms'=4,'frames'=64] {'atoms'}, use_global_device_ids=true, to_apply=%region_1.0 | all-reduce | flops 4 | bytes 32 | tf_op jit(solution)/shard_map/psum | solution.py:44
  20.2 0.8 broadcast_divide_fusion.2
  21.0 16.9 %convolution_bitcast_fusion.1 = f32[24,3,3]{0,1,2:T(4,128)S(1)} fusion(f32[24,3,24576]{2,0,1:T(8,128)} %param.4, f32[3,24576]{1,0:T(4,128)} %param.5, f32[3]{0:T(128)S(1)} %broadcast_divide_fusion.2, f32[24576]{0:T(1024)} %param.6), kind=kOutput, calls=%fused_computation.12 | convolution fusion | flops 63848448 | bytes 7471980 | tf_op jit(solution)/shard_map/ia,fja->fij/dot_general | solution.py:47
  38.0 13.8 %fusion.34 = f32[1,24,3]{1,0,2:T(1,128)S(1)} fusion(f32[24576,1,1]{0,1,2:T(1,128)S(1)} %bitcast.242, f32[24,3,24576]{2,0,1:T(8,128)S(1)} %copy-done), kind=kOutput, calls=%fused_computation.168 | convolution fusion | flops 21233664 | bytes 7176480 | tf_op jit(solution)/shard_map/a,fia->fi/dot_general | solution.py:43
  51.8 11.1 %all-reduce = (f32[24,3,3]{0,1,2:T(4,128)S(1)}, f32[24,3]{1,0:T(8,128)S(1)}) all-reduce(f32[24,3,3]{0,1,2:T(4,128)S(1)} %convolution_bitcast_fusion.1, f32[24,3]{1,0:T(8,128)S(1)} %bitcast.243), channel_id=1, replica_groups=mesh['atoms'=4,'frames'=64] {'atoms'}, use_global_device_ids=true, to_apply=%region_4.0 | all-reduce | flops 288 | bytes 2304 | tf_op jit(solution)/shard_map/psum | solution.py:48
  62.9 0.7 fusion.32
  63.6 0.7 sqrt_multiply_fusion
  65.5 0.1 broadcast_subtract_fusion
  65.8 0.1 copy.62
  65.9 0.7 broadcast_divide_fusion
  66.6 0.3 fusion.35
  66.9 29.3 %convert_reduce_fusion = (f32[3,24576]{1,0:T(4,128)S(1)}, bf16[24,3,24576]{2,1,0:T(4,128)(2,1)S(1)}) fusion(f32[3,24576]{1,0:T(4,128)S(1)} %broadcast_subtract_fusion, f32[24,3]{1,0:T(8,128)S(1)} %bitcast.269, f32[24,3,3]{2,1,0:T(4,128)S(1)} %copy.62, f32[24,3,24576]{2,0,1:T(8,128)} %param.4), kind=kOutput, calls=%fused_computation.5 | convolution fusion | flops 72474624 | bytes 11207808 | tf_op jit(solution)/shard_map/fij,fja->fia/dot_general | solution.py:53
  96.2 2.1 copy-done.1
  98.3 5.1 %fusion.33 = (f32[32]{0:T(128)S(1)}, f32[24,32]{1,0:T(8,128)S(1)}) fusion(bf16[32,3,24576]{2,0,1:T(8,128)(2,1)S(1)} %bitcast.241, bf16[24,3,24576]{2,1,0:T(4,128)(2,1)S(1)} %get-tuple-element.88), kind=kOutput, calls=%fused_computation.166 | convolution fusion | flops 113246944 | bytes 8260736 | tf_op jit(solution)/shard_map/fc,kc->fk/dot_general | solution.py:58
  103.5 12.2 %psum.53 = f32[24,32]{1,0:T(8,128)S(1)} all-reduce(f32[24,32]{1,0:T(8,128)S(1)} %get-tuple-element.90), channel_id=1, replica_groups=mesh['atoms'=4,'frames'=64] {'atoms'}, use_global_device_ids=true, to_apply=%region_7.0 | all-reduce | flops 768 | bytes 6144 | tf_op jit(solution)/shard_map/psum | solution.py:64
  115.7 87.8 %psum.54 = f32[32]{0:T(128)S(1)} all-reduce(f32[32]{0:T(128)S(1)} %get-tuple-element.89), channel_id=1, replica_groups=mesh['atoms'=4,'frames'=64] {'atoms','frames'}, use_global_device_ids=true, to_apply=%region_9.0 | all-reduce | flops 32 | bytes 256 | tf_op jit(solution)/shard_map/psum | solution.py:65
  203.4 0.2 broadcast_in_dim.3
  203.6 9.0 %fusion.3 = f32[32,3,24576]{2,0,1:T(8,128)S(1)} fusion(bf16[24,3,24576]{2,1,0:T(4,128)(2,1)} %copy-done.1, f32[24,32]{1,0:T(8,128)S(1)} %psum.53, f32[32]{0:T(128)S(1)} %broadcast_multiply_fusion.1), kind=kOutput, calls=%fused_computation.6 | convolution fusion | flops 113247744 | bytes 12979328 | tf_op jit(solution)/shard_map/fk,fia->kia/dot_general | solution.py:67
  212.6 5.7 %pad_maximum_fusion = f32[33,3,24576]{2,0,1:T(8,128)} fusion(f32[1,3,24576]{2,0,1:T(1,128)S(1)} %broadcast_in_dim.3, f32[32,3,24576]{2,0,1:T(8,128)S(1)} %fusion.3), kind=kLoop, calls=%fused_computation.3 | loop fusion | flops 2433024 | bytes 19464192 | tf_op jit(solution)/shard_map/concatenate | solution.py:71
  218.3 144.5 %reduce-scatter.2.cloned.1.call-done = f32[33,3,384]{2,0,1:T(8,128)} async-done(((f32[33,3,24576]{2,0,1:T(8,128)}), f32[33,3,384]{2,0,1:T(8,128)}) %reduce-scatter.2.cloned.1.call-update) | async-done | bytes 152080 | tf_op jit(solution)/shard_map/reduce_scatter | solution.py:72
  362.8 0.9 slice_multiply_fusion
  363.7 0.3 convolution_bitcast_fusion
  364.0 78.6 %psum.55 = f32[32,32]{0,1:T(8,128)S(1)} all-reduce(f32[32,32]{0,1:T(8,128)S(1)} %convolution_bitcast_fusion), channel_id=1, replica_groups=mesh['atoms'=4,'frames'=64] {'atoms','frames'}, use_global_device_ids=true, to_apply=%region_12.0 | all-reduce | flops 1024 | bytes 8192 | tf_op jit(solution)/shard_map/psum | solution.py:80
  442.7 2.9 cholesky.16
  445.6 0.6 compare_reduce_fusion
  446.3 0.7 fusion.18
  446.9 2.4 custom-call.7
  449.4 0.8 slice_multiply_fusion.1
  450.2 0.6 bitcast_add_fusion.1
  450.8 1.9 fusion.15
  (94 shorter events, 1.2 us)
Async XLA Ops:
  7.2 30.8 %copy-start.3 = (f32[24576]{0:T(1024)S(1)}, f32[24576]{0:T(1024)}, u32[]{:S(2)}) copy-start(f32[24576]{0:T(1024)} %param.6) | copy-start | bytes 294916
  7.2 355.6 %reduce-scatter.2.cloned.1.call-start = ((), (), s32[]{:S(2)}) async-start(), calls=%async_computation.1 | async-start | bytes 11980800 | tf_op jit(solution)/shard_map/reduce_scatter | solution.py:72
  20.2 17.7 %copy-start = (f32[24,3,24576]{2,0,1:T(8,128)S(1)}, f32[24,3,24576]{2,0,1:T(8,128)}, u32[]{:S(2)}) copy-start(f32[24,3,24576]{2,0,1:T(8,128)} %param.4) | copy-start | bytes 21233668
  21.0 44.4 %copy-start.2 = (f32[3,24576]{1,0:T(4,128)S(1)}, f32[3,24576]{1,0:T(4,128)}, u32[]{:S(2)}) copy-start(f32[3,24576]{1,0:T(4,128)} %param.5) | copy-start | bytes 884740
  65.5 32.9 %slice-start = ((s8[4718592]{0:T(1024)(128)(4,1)}), s8[524288]{0:T(1024)(128)(4,1)S(1)}, s32[]{:S(2)}) async-start(s8[4718592]{0:T(1024)(128)(4,1)} %bitcast.240), calls=%async_computation.2 | async-start | bytes 1048576
  66.9 31.5 %slice-start.1 = ((s8[4718592]{0:T(1024)(128)(4,1)}), s8[4194304]{0:T(1024)(128)(4,1)S(1)}, s32[]{:S(2)}) async-start(s8[4718592]{0:T(1024)(128)(4,1)} %bitcast.240), calls=%async_computation.3 | async-start | bytes 8388608
  96.2 2.1 copy-start.1
  363.7 89.0 %copy-start.4 = (f32[32,3,384]{2,0,1:T(8,128)}, f32[32,3,384]{2,0,1:T(8,128)S(1)}, u32[]{:S(2)}) copy-start(f32[32,3,384]{2,0,1:T(8,128)S(1)} %slice_multiply_fusion) | copy-start | bytes 442372
Sparse Core Ops, SparseCore 0:
  218.4 144.3 reduce-scatter.1
where the time goes:
time: 464 us; the launch traced here: 460 us
  blocking collectives  200 us (43%)
  waiting for transfers between devices  144 us (31%)
  matrix products  76.6 us (17%)
  other arithmetic  21.2 us (5%)
  between operations  14.9 us (3%)
    reduce_scatter x1, waiting for transfers between devices, per_device(): lax.psum_scatter(stacked, 'frames', scatter_dimension=2, tiled=True)  144 us
    psum x1, blocking collectives, per_device(): proj_total = lax.psum(jnp.sum(local_proj, axis=0), ('atoms', 'frames'))  87.8 us
    psum x1, blocking collectives, per_device(): lax.psum(jnp.dot(flat, flat.T, precision=highest), ('atoms', 'frames'))  78.6 us
    dot_general x1, matrix products, per_device(): moved = jnp.einsum('fij,fja->fia', rotation, frames, precision=highest)  29.3 us
    dot_general x1, matrix products, per_device(): jnp.einsum('ia,fja->fij', centered, frames, precision=highest)  16.9 us
    dot_general x1, matrix products, per_device(): jnp.einsum('a,fia->fi', atom_weight, frames, precision=highest)  13.8 us
    psum x1, blocking collectives, per_device(): projection = lax.psum(local_proj, 'atoms')  12.2 us
    psum x1, blocking collectives, per_device(): first, second = lax.psum((local_first, local_second), 'atoms')  11.1 us
  transfers between devices with their start and end apart: 1, of which 1 were waited for; matrix products, arithmetic and copies ran while one was open for 0% of the time, Pallas kernels for 0%

commit v1 on v0

--- a/solution.py
+++ b/solution.py
@@ -77,7 +77,10 @@
     own_mean = lax.dynamic_slice_in_dim(mean_structure, lax.axis_index("frames") * width, width, 1)
     new_mean = own_mean + mean_shift / frame_count
     flat = image.reshape(vectors, -1)
-    gram = lax.psum(jnp.dot(flat, flat.T, precision=highest), ("atoms", "frames")) / (3 * A)
+    gram = jax.lax.psum(
+        jax.lax.psum(jnp.dot(flat, flat.T, precision=highest), axis_name="frames"),
+        axis_name="atoms",
+    ) / (3 * A)
     lower = jnp.linalg.cholesky(gram)
     basis = jax.scipy.linalg.solve_triangular(lower, flat, lower=True)
     return (new_mean, image, basis.reshape(image.shape))

time: 464 us -> 650 us (1.40)
  blocking collectives: 200 us -> 380 us
    psum x1 -> x2, blocking collectives: 78.6 us -> 259 us  [the longest x1 245 us: per_device(): jax.lax.psum(jnp.dot(flat, flat.T, precision=highest), axis_name='frames')]
where the time goes in v1:
time: 650 us; the launch traced here: 640 us
  blocking collectives  380 us (58%)
  waiting for transfers between devices  145 us (22%)
  matrix products  76.3 us (12%)
  other arithmetic  21.2 us (3%)
  between operations  14.9 us (2%)
    psum x1, blocking collectives, per_device(): jax.lax.psum(jnp.dot(flat, flat.T, precision=highest), axis_name='frames')  245 us
    reduce_scatter x1, waiting for transfers between devices, per_device(): lax.psum_scatter(stacked, 'frames', scatter_dimension=2, tiled=True)  144 us
    psum x1, blocking collectives, per_device(): proj_total = lax.psum(jnp.sum(local_proj, axis=0), ('atoms', 'frames'))  87.7 us
    dot_general x1, matrix products, per_device(): moved = jnp.einsum('fij,fja->fia', rotation, frames, precision=highest)  29.3 us
    dot_general x1, matrix products, per_device(): jnp.einsum('ia,fja->fij', centered, frames, precision=highest)  16.7 us
    dot_general x1, matrix products, per_device(): jnp.einsum('a,fia->fi', atom_weight, frames, precision=highest)  13.8 us
    psum x1, blocking collectives, per_device(): jax.lax.psum(jax.lax.psum(jnp.dot(flat, flat.T, precision=highest), axis_...  13.4 us
  transfers between devices with their start and end apart: 1, of which 1 were waited for; matrix products, arithmetic and copies ran while one was open for 0% of the time, Pallas kernels for 0%

profile of v1, /device:TPU:1, one launch (start us, length us, event | category | flops | bytes accessed | tf_op | source)
XLA Modules:
  0.0 639.7 jit_solution(10879651342355483180)
XLA Ops:
  7.2 1.3 multiply_reduce_fusion
  8.6 1.5 reduce_sum.46
  10.1 10.1 %all-reduce.1 = (f32[3]{0:T(128)S(1)}, f32[]{:T(128)}) all-reduce(f32[3]{0:T(128)S(1)} %multiply_reduce_fusion, f32[]{:T(128)} %reduce_sum.46), channel_id=1, replica_groups=mesh['atoms'=4,'frames'=64] {'atoms'}, use_global_device_ids=true, to_apply=%region_1.0 | all-reduce | flops 4 | bytes 32 | tf_op jit(solution)/shard_map/psum | solution.py:44
  20.2 0.8 broadcast_divide_fusion.2
  21.0 16.7 %convolution_bitcast_fusion.1 = f32[24,3,3]{0,1,2:T(4,128)S(1)} fusion(f32[24,3,24576]{2,0,1:T(8,128)} %param.4, f32[3,24576]{1,0:T(4,128)} %param.5, f32[3]{0:T(128)S(1)} %broadcast_divide_fusion.2, f32[24576]{0:T(1024)} %param.6), kind=kOutput, calls=%fused_computation.12 | convolution fusion | flops 63848448 | bytes 7471980 | tf_op jit(solution)/shard_map/ia,fja->fij/dot_general | solution.py:47
  37.8 13.8 %fusion.34 = f32[1,24,3]{1,0,2:T(1,128)S(1)} fusion(f32[24576,1,1]{0,1,2:T(1,128)S(1)} %bitcast.242, f32[24,3,24576]{2,0,1:T(8,128)S(1)} %copy-done), kind=kOutput, calls=%fused_computation.168 | convolution fusion | flops 21233664 | bytes 7176480 | tf_op jit(solution)/shard_map/a,fia->fi/dot_general | solution.py:43
  51.6 11.4 %all-reduce = (f32[24,3,3]{0,1,2:T(4,128)S(1)}, f32[24,3]{1,0:T(8,128)S(1)}) all-reduce(f32[24,3,3]{0,1,2:T(4,128)S(1)} %convolution_bitcast_fusion.1, f32[24,3]{1,0:T(8,128)S(1)} %bitcast.243), channel_id=1, replica_groups=mesh['atoms'=4,'frames'=64] {'atoms'}, use_global_device_ids=true, to_apply=%region_4.0 | all-reduce | flops 288 | bytes 2304 | tf_op jit(solution)/shard_map/psum | solution.py:48
  63.0 0.7 fusion.32
  63.7 0.7 sqrt_multiply_fusion
  65.6 0.1 broadcast_subtract_fusion
  66.0 0.7 broadcast_divide_fusion
  66.6 0.3 fusion.35
  67.0 29.3 %convert_reduce_fusion = (f32[3,24576]{1,0:T(4,128)S(1)}, bf16[24,3,24576]{2,1,0:T(4,128)(2,1)S(1)}) fusion(f32[3,24576]{1,0:T(4,128)S(1)} %broadcast_subtract_fusion, f32[24,3]{1,0:T(8,128)S(1)} %bitcast.269, f32[24,3,3]{2,1,0:T(4,128)S(1)} %copy.62, f32[24,3,24576]{2,0,1:T(8,128)} %param.4), kind=kOutput, calls=%fused_computation.5 | convolution fusion | flops 72474624 | bytes 11207808 | tf_op jit(solution)/shard_map/fij,fja->fia/dot_general | solution.py:53
  96.3 2.1 copy-done.1
  98.4 5.1 fusion.33
  103.5 12.2 %psum.60 = f32[24,32]{1,0:T(8,128)S(1)} all-reduce(f32[24,32]{1,0:T(8,128)S(1)} %get-tuple-element.90), channel_id=1, replica_groups=mesh['atoms'=4,'frames'=64] {'atoms'}, use_global_device_ids=true, to_apply=%region_7.0 | all-reduce | flops 768 | bytes 6144 | tf_op jit(solution)/shard_map/psum | solution.py:64
  115.7 87.7 %psum.61 = f32[32]{0:T(128)S(1)} all-reduce(f32[32]{0:T(128)S(1)} %get-tuple-element.89), channel_id=1, replica_groups=mesh['atoms'=4,'frames'=64] {'atoms','frames'}, use_global_device_ids=true, to_apply=%region_9.0 | all-reduce | flops 32 | bytes 256 | tf_op jit(solution)/shard_map/psum | solution.py:65
  203.5 0.2 broadcast_in_dim.3
  203.7 9.0 %fusion.3 = f32[32,3,24576]{2,0,1:T(8,128)S(1)} fusion(bf16[24,3,24576]{2,1,0:T(4,128)(2,1)} %copy-done.1, f32[24,32]{1,0:T(8,128)S(1)} %psum.60, f32[32]{0:T(128)S(1)} %broadcast_multiply_fusion.1), kind=kOutput, calls=%fused_computation.6 | convolution fusion | flops 113247744 | bytes 12979328 | tf_op jit(solution)/shard_map/fk,fia->kia/dot_general | solution.py:67
  212.6 5.7 pad_maximum_fusion
  218.3 144.5 %reduce-scatter.2.cloned.1.call-done = f32[33,3,384]{2,0,1:T(8,128)} async-done(((f32[33,3,24576]{2,0,1:T(8,128)}), f32[33,3,384]{2,0,1:T(8,128)}) %reduce-scatter.2.cloned.1.call-update) | async-done | bytes 152080 | tf_op jit(solution)/shard_map/reduce_scatter | solution.py:72
  362.8 0.9 slice_multiply_fusion
  363.8 0.3 convolution_bitcast_fusion
  364.0 245.2 %psum.62 = f32[32,32]{0,1:T(8,128)S(1)} all-reduce(f32[32,32]{0,1:T(8,128)S(1)} %convolution_bitcast_fusion), channel_id=1, replica_groups=mesh['atoms'=4,'frames'=64] {'frames'}, use_global_device_ids=true, to_apply=%region_12.0 | all-reduce | flops 1024 | bytes 8192 | tf_op jit(solution)/shard_map/psum | solution.py:81
  609.2 13.4 %psum.63 = f32[32,32]{0,1:T(8,128)S(1)} all-reduce(f32[32,32]{0,1:T(8,128)S(1)} %psum.62), channel_id=1, replica_groups=mesh['atoms'=4,'frames'=64] {'atoms'}, use_global_device_ids=true, to_apply=%region_13.0 | all-reduce | flops 1024 | bytes 8192 | tf_op jit(solution)/shard_map/psum | solution.py:80
  622.7 2.9 cholesky.16
  625.7 0.6 compare_reduce_fusion
  626.3 0.7 fusion.18
  627.0 2.4 custom-call.7
  629.4 0.8 slice_multiply_fusion.1
  630.2 0.6 bitcast_add_fusion.1
  630.8 1.9 fusion.15
  (95 shorter events, 1.3 us)
Async XLA Ops:
  7.2 30.6 %copy-start.3 = (f32[24576]{0:T(1024)S(1)}, f32[24576]{0:T(1024)}, u32[]{:S(2)}) copy-start(f32[24576]{0:T(1024)} %param.6) | copy-start | bytes 294916
  7.2 355.7 %reduce-scatter.2.cloned.1.call-start = ((), (), s32[]{:S(2)}) async-start(), calls=%async_computation.1 | async-start | bytes 11980800 | tf_op jit(solution)/shard_map/reduce_scatter | solution.py:72
  20.2 17.5 %copy-start = (f32[24,3,24576]{2,0,1:T(8,128)S(1)}, f32[24,3,24576]{2,0,1:T(8,128)}, u32[]{:S(2)}) copy-start(f32[24,3,24576]{2,0,1:T(8,128)} %param.4) | copy-start | bytes 21233668
  21.0 44.5 %copy-start.2 = (f32[3,24576]{1,0:T(4,128)S(1)}, f32[3,24576]{1,0:T(4,128)}, u32[]{:S(2)}) copy-start(f32[3,24576]{1,0:T(4,128)} %param.5) | copy-start | bytes 884740
  65.6 32.8 %slice-start = ((s8[4718592]{0:T(1024)(128)(4,1)}), s8[524288]{0:T(1024)(128)(4,1)S(1)}, s32[]{:S(2)}) async-start(s8[4718592]{0:T(1024)(128)(4,1)} %bitcast.240), calls=%async_computation.2 | async-start | bytes 1048576
  66.9 31.4 %slice-start.1 = ((s8[4718592]{0:T(1024)(128)(4,1)}), s8[4194304]{0:T(1024)(128)(4,1)S(1)}, s32[]{:S(2)}) async-start(s8[4718592]{0:T(1024)(128)(4,1)} %bitcast.240), calls=%async_computation.3 | async-start | bytes 8388608
  96.2 2.1 copy-start.1
  363.8 269.0 %copy-start.4 = (f32[32,3,384]{2,0,1:T(8,128)}, f32[32,3,384]{2,0,1:T(8,128)S(1)}, u32[]{:S(2)}) copy-start(f32[32,3,384]{2,0,1:T(8,128)S(1)} %slice_multiply_fusion) | copy-start | bytes 442372
Sparse Core Ops, SparseCore 0:
  218.4 144.3 reduce-scatter.1
